TPU v7x, 32 devices: a whole 2x2x4 slice. The times are simulated.
32 devices in a mesh: tm: 8 (over y, x, core), rows: 4 (over z).
Axes of the slice: x: 2, y: 2, z: 4, core: 2. Of those that a mesh axis runs over, the one named last changes fastest.
Arguments:
- frames_in: bfloat16 [32, 32, 32, 512], P('tm', 'rows'), may hold values from -6 to 6
- weight_in: bfloat16 [2, 512, 4608], P(None, 'rows'), may hold values from -0.09375 to 0.09375
- weight_out: bfloat16 [9, 2, 512, 512], P(None, None, 'rows'), may hold values from -0.015625 to 0.015625
- log_decay: float32 [512], replicated, may hold values from 0.0003125 to 0.06
- rotation: float32 [512], replicated, may hold values from -3.140625 to 3.140625
- start_state: float32 [32, 32, 2, 512], P('rows'), may hold values from -12 to 12
- skip_gain: float32 [512], replicated, may hold values from -1 to 1
Outputs:
- frames_out: bfloat16 [32, 32, 32, 512], P('tm', 'rows')
All inputs are finite; a program needn't handle non-finite values.
Results may differ from a plain program's by a relative error of at most 0.0047.
Values may be sent and summed in bfloat16 or wider, within the bound.
A program may use at most 128 MiB of HBM per device.

v0:
```python
import jax
import jax.numpy as jnp
from jax import lax
from jax.sharding import PartitionSpec as P


def passed_along(value, axis, steps):
    count = lax.axis_size(axis)
    first, last = (max(0, -steps), min(count, count - steps))
    return lax.ppermute(value, axis, [(source, source + steps) for source in range(first, last)])


def extended_2(cells, sides, width):
    for axis, dim in sides:
        count = lax.axis_size(axis)
        ends = count - 1
        head = lax.slice_in_dim(cells, 0, width, axis=dim)
        tail = lax.slice_in_dim(cells, cells.shape[dim] - width, cells.shape[dim], axis=dim)
        cells = jnp.concatenate(
            [
                lax.ppermute(tail, axis, [(i, (i + 1) % count) for i in range(ends)]),
                cells,
                lax.ppermute(head, axis, [((i + 1) % count, i) for i in range(ends)]),
            ],
            axis=dim,
        )
    return cells


def pad_field(field, rows_pad):
    widths = [(0, 0)] * field.ndim
    widths[1] = (rows_pad, rows_pad)
    widths[2] = (1, 1)
    return jnp.pad(field, widths)


def in_term(padded, piece, height, columns):
    parts, state_width, span = piece.shape
    channels = span // 9
    matrix = piece.reshape(parts * state_width, span)
    summed = jnp.zeros((padded.shape[0], height, columns, parts * state_width), jnp.float32)
    for tap_index in range(9):
        row_shift = tap_index // 3
        col_shift = tap_index % 3
        window = padded[:, row_shift : row_shift + height, col_shift : col_shift + columns, :]
        weight_tap = matrix[:, tap_index * channels : (tap_index + 1) * channels]
        summed = summed + lax.dot_general(
            window, weight_tap, (((3,), (1,)), ((), ())), preferred_element_type=jnp.float32
        )
    return summed.reshape(padded.shape[0], height, columns, parts, state_width)


def out_term(padded_held, piece, height, columns):
    summed = jnp.zeros((padded_held.shape[0], height, columns, piece.shape[3]), jnp.float32)
    for tap_index in range(9):
        row_shift = tap_index // 3
        col_shift = tap_index % 3
        window = padded_held[:, row_shift : row_shift + height, col_shift : col_shift + columns]
        summed = summed + lax.dot_general(
            window,
            piece[tap_index],
            (((3, 4), (0, 1)), ((), ())),
            preferred_element_type=jnp.float32,
        )
    return summed


def run_states(driven, start_re, start_im, log_rate, angle):
    frame_count = driven.shape[0]
    modulus = jnp.exp(-log_rate)
    lam_re = modulus * jnp.cos(angle)
    lam_im = modulus * jnp.sin(angle)
    is_first = lax.axis_index("tm") == 0
    begin_re = jnp.where(is_first, start_re, jnp.float32(0.0))
    begin_im = jnp.where(is_first, start_im, jnp.float32(0.0))

    def advance(carried, forcing):
        state_re, state_im = carried
        force_re, force_im = forcing
        new_re = lam_re * state_re - lam_im * state_im + force_re
        new_im = lam_re * state_im + lam_im * state_re + force_im
        return ((new_re, new_im), (new_re, new_im))

    (tail_re, tail_im), (local_re, local_im) = lax.scan(
        advance, (begin_re, begin_im), (driven[..., 0, :], driven[..., 1, :])
    )
    span_mod = jnp.exp(-log_rate * frame_count)
    span_re = span_mod * jnp.cos(angle * frame_count)
    span_im = span_mod * jnp.sin(angle * frame_count)

    def relay(turn_index, carried):
        prior_re, prior_im = carried
        sent_re = span_re * prior_re - span_im * prior_im + tail_re
        sent_im = span_re * prior_im + span_im * prior_re + tail_im
        return passed_along((sent_re, sent_im), "tm", 1)

    carry_re, carry_im = lax.fori_loop(
        0, lax.axis_size("tm") - 1, relay, (jnp.zeros_like(tail_re), jnp.zeros_like(tail_im))
    )
    step_count = jnp.arange(1, frame_count + 1, dtype=jnp.float32)[:, None, None, None]
    power_mod = jnp.exp(-log_rate * step_count)
    power_re = power_mod * jnp.cos(angle * step_count)
    power_im = power_mod * jnp.sin(angle * step_count)
    states_re = local_re + power_re * carry_re - power_im * carry_im
    states_im = local_im + power_re * carry_im + power_im * carry_re
    return jnp.stack([states_re, states_im], 3).astype(jnp.bfloat16)


def on_device(frames_in, weight_in, weight_out, log_decay, rotation, start_state, skip_gain):
    frame_count, band_rows, columns, channels = frames_in.shape
    extended = extended_2(frames_in, (("rows", 1),), 1)
    padded = pad_field(extended, 0)
    driven = in_term(
        padded, lax.all_gather(weight_in, "rows", axis=1, tiled=True), band_rows, columns
    )
    held = run_states(driven, start_state[:, :, 0, :], start_state[:, :, 1, :], log_decay, rotation)
    held = extended_2(held, (("rows", 1),), 1)
    held_padded = pad_field(held, 0)
    mixing = out_term(
        held_padded, lax.all_gather(weight_out, "rows", axis=2, tiled=True), band_rows, columns
    )
    pre_act = mixing + skip_gain * frames_in.astype(jnp.float32)
    return jax.nn.gelu(pre_act, approximate=False).astype(jnp.bfloat16)


def solution(mesh):
    return jax.shard_map(
        on_device,
        mesh=mesh,
        in_specs=(
            P("tm", "rows", None, None),
            P(None, "rows", None),
            P(None, None, "rows", None),
            P(),
            P(),
            P("rows", None, None, None),
            P(),
        ),
        out_specs=P("tm", "rows", None, None),
        check_vma=False,
    )
```

profile of v0, /device:TPU:12, one launch (start us, length us, event | category | flops | bytes accessed | tf_op | source)
XLA Modules:
  0.0 405.1 jit_solution(16774444298382258066)
XLA Ops:
  9.0 3.5 collective-permute-start.2
  20.2 153.8 %all-gather.3.cloned.1.call-done = bf16[2,512,4608]{2,1,0:T(8,128)(2,1)} async-done(((bf16[2,128,4608]{2,1,0:T(8,128)(2,1)}), bf16[2,512,4608]{2,1,0:T(8,128)(2,1)}) %all-gather.3.cloned.1.call-update) | async-done | bytes 9437200 | tf_op jit(solution)/shard_map/all_gather | solution.py:114
  177.0 3.2 fusion.55
  180.2 3.3 fusion.63
  183.5 3.4 fusion.65
  186.8 3.3 fusion.68
  190.2 3.2 fusion.70
  193.4 3.2 fusion.72
  196.7 3.4 fusion.67
  200.0 11.9 %add_add_fusion.1 = f32[4,8,32,1024]{3,2,1,0:T(8,128)} fusion(f32[4,8,32,1024]{3,2,1,0:T(8,128)S(1)} %fusion.55, f32[4,8,32,1024]{3,2,1,0:T(8,128)} %fusion.63, f32[4,8,32,1024]{3,2,1,0:T(8,128)} %fusion.65, f32[4,8,32,1024]{3,2,1,0:T(8,128)} %fusion.67, f32[4,8,32,1024]{3,2,1,0:T(8,128)} %fusion.68, f32[4,8,32,1024]{3,2,1,0:T(8,128)} %fusion.70, ...), kind=kOutput, calls=%fused_computation.11 | convolution fusion | flops 1082130432 | bytes 39845888 | tf_op jit(solution)/shard_map/dot_general | solution.py:47
  211.9 6.6 %reshape.132 = f32[4,8,32,2,512]{4,3,2,1,0:T(2,128)} reshape(f32[4,8,32,1024]{3,2,1,0:T(8,128)} %add_add_fusion.1) | data formatting | bytes 8388608 | tf_op jit(solution)/shard_map/reshape | solution.py:50
  218.5 7.9 %fusion.83 = (f32[4,8,32,1,512]{4,3,2,1,0:T(1,128)S(1)}, f32[4,8,32,1,512]{4,3,2,1,0:T(1,128)S(1)}) fusion(f32[4,8,32,2,512]{4,3,2,1,0:T(2,128)} %reshape.132), kind=kLoop, calls=%fused_computation.146 | loop fusion | bytes 8388608 | tf_op jit(solution)/shard_map/slice | solution.py:85
  231.6 9.8 %while.28 = (s32[]{:T(128)}, f32[8,32,512]{2,1,0:T(8,128)S(1)}, f32[8,32,512]{2,1,0:T(8,128)S(1)}, f32[4,8,32,512]{3,2,1,0:T(8,128)}, f32[4,8,32,512]{3,2,1,0:T(...) while((s32[]{:T(128)}, f32[8,32,512]{2,1,0:T(8,128)S(1)}, ...), condition=%wide.region_1.2_spmd, body=%wide.region_0.1_spmd.sunk | while | flops 1048578 | bytes 4199013 | solution.py:84
  241.5 120.9 %while.29 = (s32[]{:T(128)}, f32[8,32,512]{2,1,0:T(8,128)S(1)}, f32[8,32,512]{2,1,0:T(8,128)S(1)}, f32[512]{0:T(512)S(1)}, f32[512]{0:T(512)S(1)}, /*index=5*/f3...) while((s32[]{:T(128)}, f32[8,32,512]{2,1,0:T(8,128)S(1)}, f32[8,32,512]{2,1,0:T(8,128)S(1)}, ...), condition=%wide.region_3.4_spmd, body=%wide.region_2.3_spmd.sunk | while | flops 1048578 | bytes 7344293 | solution.py:97
  243.7 3.5 collective-permute-start.1
  247.2 6.0 %collective-permute-done = f32[8,32,512]{2,1,0:T(8,128)S(1)} collective-permute-done((f32[8,32,512]{2,1,0:T(8,128)S(1)}, f32[8,32,512]{2,1,0:T(8,128)S(1)}, u32[]{:S(2)}, u32[]{:S(2)}) %collective-permute-start) | collective-permute-done | bytes 524320 | tf_op jit(solution)/shard_map/while/body/eval_jaxpr/ppermute | solution.py:10
  253.2 5.6 %collective-permute-done.1 = f32[8,32,512]{2,1,0:T(8,128)S(1)} collective-permute-done((f32[8,32,512]{2,1,0:T(8,128)S(1)}, f32[8,32,512]{2,1,0:T(8,128)S(1)}, u32[]{:S(2)}, u32[]{:S(2)}) %collective-permute-start.1) | collective-permute-done | bytes 524320 | tf_op jit(solution)/shard_map/while/body/eval_jaxpr/ppermute | solution.py:10
  263.6 6.9 %collective-permute-done = f32[8,32,512]{2,1,0:T(8,128)S(1)} collective-permute-done((f32[8,32,512]{2,1,0:T(8,128)S(1)}, f32[8,32,512]{2,1,0:T(8,128)S(1)}, u32[]{:S(2)}, u32[]{:S(2)}) %collective-permute-start) | collective-permute-done | bytes 524320 | tf_op jit(solution)/shard_map/while/body/eval_jaxpr/ppermute | solution.py:10
  270.4 5.6 %collective-permute-done.1 = f32[8,32,512]{2,1,0:T(8,128)S(1)} collective-permute-done((f32[8,32,512]{2,1,0:T(8,128)S(1)}, f32[8,32,512]{2,1,0:T(8,128)S(1)}, u32[]{:S(2)}, u32[]{:S(2)}) %collective-permute-start.1) | collective-permute-done | bytes 524320 | tf_op jit(solution)/shard_map/while/body/eval_jaxpr/ppermute | solution.py:10
  280.2 7.5 %collective-permute-done = f32[8,32,512]{2,1,0:T(8,128)S(1)} collective-permute-done((f32[8,32,512]{2,1,0:T(8,128)S(1)}, f32[8,32,512]{2,1,0:T(8,128)S(1)}, u32[]{:S(2)}, u32[]{:S(2)}) %collective-permute-start) | collective-permute-done | bytes 524320 | tf_op jit(solution)/shard_map/while/body/eval_jaxpr/ppermute | solution.py:10
  287.7 5.6 %collective-permute-done.1 = f32[8,32,512]{2,1,0:T(8,128)S(1)} collective-permute-done((f32[8,32,512]{2,1,0:T(8,128)S(1)}, f32[8,32,512]{2,1,0:T(8,128)S(1)}, u32[]{:S(2)}, u32[]{:S(2)}) %collective-permute-start.1) | collective-permute-done | bytes 524320 | tf_op jit(solution)/shard_map/while/body/eval_jaxpr/ppermute | solution.py:10
  297.4 7.5 %collective-permute-done = f32[8,32,512]{2,1,0:T(8,128)S(1)} collective-permute-done((f32[8,32,512]{2,1,0:T(8,128)S(1)}, f32[8,32,512]{2,1,0:T(8,128)S(1)}, u32[]{:S(2)}, u32[]{:S(2)}) %collective-permute-start) | collective-permute-done | bytes 524320 | tf_op jit(solution)/shard_map/while/body/eval_jaxpr/ppermute | solution.py:10
  305.0 5.6 %collective-permute-done.1 = f32[8,32,512]{2,1,0:T(8,128)S(1)} collective-permute-done((f32[8,32,512]{2,1,0:T(8,128)S(1)}, f32[8,32,512]{2,1,0:T(8,128)S(1)}, u32[]{:S(2)}, u32[]{:S(2)}) %collective-permute-start.1) | collective-permute-done | bytes 524320 | tf_op jit(solution)/shard_map/while/body/eval_jaxpr/ppermute | solution.py:10
  314.7 7.5 %collective-permute-done = f32[8,32,512]{2,1,0:T(8,128)S(1)} collective-permute-done((f32[8,32,512]{2,1,0:T(8,128)S(1)}, f32[8,32,512]{2,1,0:T(8,128)S(1)}, u32[]{:S(2)}, u32[]{:S(2)}) %collective-permute-start) | collective-permute-done | bytes 524320 | tf_op jit(solution)/shard_map/while/body/eval_jaxpr/ppermute | solution.py:10
  322.3 5.6 %collective-permute-done.1 = f32[8,32,512]{2,1,0:T(8,128)S(1)} collective-permute-done((f32[8,32,512]{2,1,0:T(8,128)S(1)}, f32[8,32,512]{2,1,0:T(8,128)S(1)}, u32[]{:S(2)}, u32[]{:S(2)}) %collective-permute-start.1) | collective-permute-done | bytes 524320 | tf_op jit(solution)/shard_map/while/body/eval_jaxpr/ppermute | solution.py:10
  332.0 7.5 %collective-permute-done = f32[8,32,512]{2,1,0:T(8,128)S(1)} collective-permute-done((f32[8,32,512]{2,1,0:T(8,128)S(1)}, f32[8,32,512]{2,1,0:T(8,128)S(1)}, u32[]{:S(2)}, u32[]{:S(2)}) %collective-permute-start) | collective-permute-done | bytes 524320 | tf_op jit(solution)/shard_map/while/body/eval_jaxpr/ppermute | solution.py:10
  339.5 5.6 %collective-permute-done.1 = f32[8,32,512]{2,1,0:T(8,128)S(1)} collective-permute-done((f32[8,32,512]{2,1,0:T(8,128)S(1)}, f32[8,32,512]{2,1,0:T(8,128)S(1)}, u32[]{:S(2)}, u32[]{:S(2)}) %collective-permute-start.1) | collective-permute-done | bytes 524320 | tf_op jit(solution)/shard_map/while/body/eval_jaxpr/ppermute | solution.py:10
  349.3 7.5 %collective-permute-done = f32[8,32,512]{2,1,0:T(8,128)S(1)} collective-permute-done((f32[8,32,512]{2,1,0:T(8,128)S(1)}, f32[8,32,512]{2,1,0:T(8,128)S(1)}, u32[]{:S(2)}, u32[]{:S(2)}) %collective-permute-start) | collective-permute-done | bytes 524320 | tf_op jit(solution)/shard_map/while/body/eval_jaxpr/ppermute | solution.py:10
  356.8 5.6 %collective-permute-done.1 = f32[8,32,512]{2,1,0:T(8,128)S(1)} collective-permute-done((f32[8,32,512]{2,1,0:T(8,128)S(1)}, f32[8,32,512]{2,1,0:T(8,128)S(1)}, u32[]{:S(2)}, u32[]{:S(2)}) %collective-permute-start.1) | collective-permute-done | bytes 524320 | tf_op jit(solution)/shard_map/while/body/eval_jaxpr/ppermute | solution.py:10
  365.5 4.4 %collective-permute-start.4 = (bf16[4,1,32,2,512]{4,2,3,1,0:T(8,128)(2,1)S(1)}, bf16[4,1,32,2,512]{4,2,3,1,0:T(8,128)(2,1)S(1)}, u32[]{:S(2)}, u32[]{:S(2)}) collective-permute-start(bf16[4,1,32,2,512]{4,2,3,1,0:T(8,128)(2,1)S(1)} %get-tuple-element.141), channel_id=1, source_target_pairs={{0,1},{1,2},{2,3},{4,5},{5,6},{6,7},{8,9},{9,10},{10,11},{12,13},{... | collective-permute-start | bytes 786440 | tf_op jit(solution)/shard_map/ppermute | solution.py:21
  374.9 3.9 fusion.5
  389.6 8.6 %fusion.19 = bf16[4,8,32,512]{3,2,1,0:T(8,128)(2,1)} fusion(bf16[4,8,32,512]{3,2,1,0:T(8,128)(2,1)S(1)} %copy-done.2, f32[4,8,32,512,1]{3,2,4,1,0:T(8,128)} %fusion.11, f32[4,8,32,512,1]{3,2,4,1,0:T(8,128)S(1)} %fusion.22, f32[4,8,32,512,1]{3,2,4,1,0:T(8,128)S(1)} %fusion.24, f32[4,8,32,512,1]{3,2,4,1,0:T(8,128)S(1)} %fusion.32, ...), kind=kOutput, calls=%fused_computation.33 | convolution fusion | flops 1113587712 | bytes 22022144 | tf_op jit(solution)/shard_map/dot_general | solution.py:59
  (81 shorter events, 74.3 us)
Async XLA Ops:
  6.5 8.4 %copy-start.6 = (f32[512]{0:T(512)S(1)}, f32[512]{0:T(512)}, u32[]{:S(2)}) copy-start(f32[512]{0:T(512)} %param.14) | copy-start | bytes 6148
  6.5 8.4 %copy-start.5 = (f32[512]{0:T(512)S(1)}, f32[512]{0:T(512)}, u32[]{:S(2)}) copy-start(f32[512]{0:T(512)} %param.15) | copy-start | bytes 6148
  6.5 8.4 %copy-start.4 = (f32[8,32,2,512]{3,2,1,0:T(2,128)S(1)}, f32[8,32,2,512]{3,2,1,0:T(2,128)}, u32[]{:S(2)}) copy-start(f32[8,32,2,512]{3,2,1,0:T(2,128)} %param.16) | copy-start | bytes 3145732
  6.5 167.5 %all-gather.3.cloned.1.call-start = ((), (), s32[]{:S(2)}) async-start(), calls=%async_computation | async-start | bytes 11796480 | tf_op jit(solution)/shard_map/all_gather | solution.py:114
  7.3 365.0 %all-gather.5.cloned.1.call-start = ((), (), s32[]{:S(2)}) async-start(), calls=%async_computation.1 | async-start | bytes 11796480 | tf_op jit(solution)/shard_map/all_gather | solution.py:120
  9.0 7.3 %collective-permute-start.2 = (bf16[4,1,32,512]{3,2,1,0:T(8,128)(2,1)S(1)}, bf16[4,1,32,512]{3,2,1,0:T(8,128)(2,1)S(1)}, u32[]{:S(2)}, u32[]{:S(2)}) collective-permute-start(bf16[4,1,32,512]{3,2,1,0:T(8,128)(2,1)S(1)} %get-tuple-element.145), channel_id=1, source_target_pairs={{0,1},{1,2},{2,3},{4,5},{5,6},{6,7},{8,9},{9,10},{10,11},{12,13},{... | collective-permute-start | bytes 393224 | tf_op jit(solution)/shard_map/ppermute | solution.py:21
  12.5 6.9 %collective-permute-start.3 = (bf16[4,1,32,512]{3,2,1,0:T(8,128)(2,1)S(1)}, bf16[4,1,32,512]{3,2,1,0:T(8,128)(2,1)S(1)}, u32[]{:S(2)}, u32[]{:S(2)}) collective-permute-start(bf16[4,1,32,512]{3,2,1,0:T(8,128)(2,1)S(1)} %get-tuple-element.146), channel_id=1, source_target_pairs={{1,0},{2,1},{3,2},{5,4},{6,5},{7,6},{9,8},{10,9},{11,10},{13,12},{... | collective-permute-start | bytes 393224 | tf_op jit(solution)/shard_map/ppermute | solution.py:23
  15.0 4.4 %copy-start = (bf16[4,8,32,512]{3,2,1,0:T(8,128)(2,1)S(1)}, bf16[4,8,32,512]{3,2,1,0:T(8,128)(2,1)}, u32[]{:S(2)}) copy-start(bf16[4,8,32,512]{3,2,1,0:T(8,128)(2,1)} %param.11) | copy-start | bytes 3145732
  174.1 2.9 copy-start.1
  174.1 6.1 %copy-start.3 = (bf16[2,512,4608]{2,1,0:T(8,128)(2,1)S(1)}, bf16[2,512,4608]{2,1,0:T(8,128)(2,1)}, u32[]{:S(2)}) copy-start(bf16[2,512,4608]{2,1,0:T(8,128)(2,1)} %all-gather.3.cloned.1.call-done) | copy-start | bytes 28311556
  241.8 11.4 %collective-permute-start = (f32[8,32,512]{2,1,0:T(8,128)S(1)}, f32[8,32,512]{2,1,0:T(8,128)S(1)}, u32[]{:S(2)}, u32[]{:S(2)}) collective-permute-start(f32[8,32,512]{2,1,0:T(8,128)S(1)} %get-tuple-element.268), channel_id=1, source_target_pairs={{0,4},{4,8},{8,12},{12,16},{16,20},{20,24},{24,28},{1,5},{5,9},{9,... | collective-permute-start | bytes 1572872 | tf_op jit(solution)/shard_map/while/body/eval_jaxpr/ppermute | solution.py:10
  243.7 15.1 %collective-permute-start.1 = (f32[8,32,512]{2,1,0:T(8,128)S(1)}, f32[8,32,512]{2,1,0:T(8,128)S(1)}, u32[]{:S(2)}, u32[]{:S(2)}) collective-permute-start(f32[8,32,512]{2,1,0:T(8,128)S(1)} %get-tuple-element.269), channel_id=1, source_target_pairs={{0,4},{4,8},{8,12},{12,16},{16,20},{20,24},{24,28},{1,5},{5,9},{9,... | collective-permute-start | bytes 1572872 | tf_op jit(solution)/shard_map/while/body/eval_jaxpr/ppermute | solution.py:10
  259.0 11.4 %collective-permute-start = (f32[8,32,512]{2,1,0:T(8,128)S(1)}, f32[8,32,512]{2,1,0:T(8,128)S(1)}, u32[]{:S(2)}, u32[]{:S(2)}) collective-permute-start(f32[8,32,512]{2,1,0:T(8,128)S(1)} %get-tuple-element.268), channel_id=1, source_target_pairs={{0,4},{4,8},{8,12},{12,16},{16,20},{20,24},{24,28},{1,5},{5,9},{9,... | collective-permute-start | bytes 1572872 | tf_op jit(solution)/shard_map/while/body/eval_jaxpr/ppermute | solution.py:10
  261.0 15.1 %collective-permute-start.1 = (f32[8,32,512]{2,1,0:T(8,128)S(1)}, f32[8,32,512]{2,1,0:T(8,128)S(1)}, u32[]{:S(2)}, u32[]{:S(2)}) collective-permute-start(f32[8,32,512]{2,1,0:T(8,128)S(1)} %get-tuple-element.269), channel_id=1, source_target_pairs={{0,4},{4,8},{8,12},{12,16},{16,20},{20,24},{24,28},{1,5},{5,9},{9,... | collective-permute-start | bytes 1572872 | tf_op jit(solution)/shard_map/while/body/eval_jaxpr/ppermute | solution.py:10
  276.3 11.4 %collective-permute-start = (f32[8,32,512]{2,1,0:T(8,128)S(1)}, f32[8,32,512]{2,1,0:T(8,128)S(1)}, u32[]{:S(2)}, u32[]{:S(2)}) collective-permute-start(f32[8,32,512]{2,1,0:T(8,128)S(1)} %get-tuple-element.268), channel_id=1, source_target_pairs={{0,4},{4,8},{8,12},{12,16},{16,20},{20,24},{24,28},{1,5},{5,9},{9,... | collective-permute-start | bytes 1572872 | tf_op jit(solution)/shard_map/while/body/eval_jaxpr/ppermute | solution.py:10
  278.2 15.1 %collective-permute-start.1 = (f32[8,32,512]{2,1,0:T(8,128)S(1)}, f32[8,32,512]{2,1,0:T(8,128)S(1)}, u32[]{:S(2)}, u32[]{:S(2)}) collective-permute-start(f32[8,32,512]{2,1,0:T(8,128)S(1)} %get-tuple-element.269), channel_id=1, source_target_pairs={{0,4},{4,8},{8,12},{12,16},{16,20},{20,24},{24,28},{1,5},{5,9},{9,... | collective-permute-start | bytes 1572872 | tf_op jit(solution)/shard_map/while/body/eval_jaxpr/ppermute | solution.py:10
  293.6 11.4 %collective-permute-start = (f32[8,32,512]{2,1,0:T(8,128)S(1)}, f32[8,32,512]{2,1,0:T(8,128)S(1)}, u32[]{:S(2)}, u32[]{:S(2)}) collective-permute-start(f32[8,32,512]{2,1,0:T(8,128)S(1)} %get-tuple-element.268), channel_id=1, source_target_pairs={{0,4},{4,8},{8,12},{12,16},{16,20},{20,24},{24,28},{1,5},{5,9},{9,... | collective-permute-start | bytes 1572872 | tf_op jit(solution)/shard_map/while/body/eval_jaxpr/ppermute | solution.py:10
  295.5 15.1 %collective-permute-start.1 = (f32[8,32,512]{2,1,0:T(8,128)S(1)}, f32[8,32,512]{2,1,0:T(8,128)S(1)}, u32[]{:S(2)}, u32[]{:S(2)}) collective-permute-start(f32[8,32,512]{2,1,0:T(8,128)S(1)} %get-tuple-element.269), channel_id=1, source_target_pairs={{0,4},{4,8},{8,12},{12,16},{16,20},{20,24},{24,28},{1,5},{5,9},{9,... | collective-permute-start | bytes 1572872 | tf_op jit(solution)/shard_map/while/body/eval_jaxpr/ppermute | solution.py:10
  310.9 11.4 %collective-permute-start = (f32[8,32,512]{2,1,0:T(8,128)S(1)}, f32[8,32,512]{2,1,0:T(8,128)S(1)}, u32[]{:S(2)}, u32[]{:S(2)}) collective-permute-start(f32[8,32,512]{2,1,0:T(8,128)S(1)} %get-tuple-element.268), channel_id=1, source_target_pairs={{0,4},{4,8},{8,12},{12,16},{16,20},{20,24},{24,28},{1,5},{5,9},{9,... | collective-permute-start | bytes 1572872 | tf_op jit(solution)/shard_map/while/body/eval_jaxpr/ppermute | solution.py:10
  312.8 15.1 %collective-permute-start.1 = (f32[8,32,512]{2,1,0:T(8,128)S(1)}, f32[8,32,512]{2,1,0:T(8,128)S(1)}, u32[]{:S(2)}, u32[]{:S(2)}) collective-permute-start(f32[8,32,512]{2,1,0:T(8,128)S(1)} %get-tuple-element.269), channel_id=1, source_target_pairs={{0,4},{4,8},{8,12},{12,16},{16,20},{20,24},{24,28},{1,5},{5,9},{9,... | collective-permute-start | bytes 1572872 | tf_op jit(solution)/shard_map/while/body/eval_jaxpr/ppermute | solution.py:10
  328.1 11.4 %collective-permute-start = (f32[8,32,512]{2,1,0:T(8,128)S(1)}, f32[8,32,512]{2,1,0:T(8,128)S(1)}, u32[]{:S(2)}, u32[]{:S(2)}) collective-permute-start(f32[8,32,512]{2,1,0:T(8,128)S(1)} %get-tuple-element.268), channel_id=1, source_target_pairs={{0,4},{4,8},{8,12},{12,16},{16,20},{20,24},{24,28},{1,5},{5,9},{9,... | collective-permute-start | bytes 1572872 | tf_op jit(solution)/shard_map/while/body/eval_jaxpr/ppermute | solution.py:10
  330.1 15.1 %collective-permute-start.1 = (f32[8,32,512]{2,1,0:T(8,128)S(1)}, f32[8,32,512]{2,1,0:T(8,128)S(1)}, u32[]{:S(2)}, u32[]{:S(2)}) collective-permute-start(f32[8,32,512]{2,1,0:T(8,128)S(1)} %get-tuple-element.269), channel_id=1, source_target_pairs={{0,4},{4,8},{8,12},{12,16},{16,20},{20,24},{24,28},{1,5},{5,9},{9,... | collective-permute-start | bytes 1572872 | tf_op jit(solution)/shard_map/while/body/eval_jaxpr/ppermute | solution.py:10
  345.4 11.4 %collective-permute-start = (f32[8,32,512]{2,1,0:T(8,128)S(1)}, f32[8,32,512]{2,1,0:T(8,128)S(1)}, u32[]{:S(2)}, u32[]{:S(2)}) collective-permute-start(f32[8,32,512]{2,1,0:T(8,128)S(1)} %get-tuple-element.268), channel_id=1, source_target_pairs={{0,4},{4,8},{8,12},{12,16},{16,20},{20,24},{24,28},{1,5},{5,9},{9,... | collective-permute-start | bytes 1572872 | tf_op jit(solution)/shard_map/while/body/eval_jaxpr/ppermute | solution.py:10
  347.3 15.1 %collective-permute-start.1 = (f32[8,32,512]{2,1,0:T(8,128)S(1)}, f32[8,32,512]{2,1,0:T(8,128)S(1)}, u32[]{:S(2)}, u32[]{:S(2)}) collective-permute-start(f32[8,32,512]{2,1,0:T(8,128)S(1)} %get-tuple-element.269), channel_id=1, source_target_pairs={{0,4},{4,8},{8,12},{12,16},{16,20},{20,24},{24,28},{1,5},{5,9},{9,... | collective-permute-start | bytes 1572872 | tf_op jit(solution)/shard_map/while/body/eval_jaxpr/ppermute | solution.py:10
  365.5 9.4 %collective-permute-start.4 = (bf16[4,1,32,2,512]{4,2,3,1,0:T(8,128)(2,1)S(1)}, bf16[4,1,32,2,512]{4,2,3,1,0:T(8,128)(2,1)S(1)}, u32[]{:S(2)}, u32[]{:S(2)}) collective-permute-start(bf16[4,1,32,2,512]{4,2,3,1,0:T(8,128)(2,1)S(1)} %get-tuple-element.141), channel_id=1, source_target_pairs={{0,1},{1,2},{2,3},{4,5},{5,6},{6,7},{8,9},{9,10},{10,11},{12,13},{... | collective-permute-start | bytes 786440 | tf_op jit(solution)/shard_map/ppermute | solution.py:21
  369.9 9.0 %collective-permute-start.5 = (bf16[4,1,32,2,512]{4,2,3,1,0:T(8,128)(2,1)S(1)}, bf16[4,1,32,2,512]{4,2,3,1,0:T(8,128)(2,1)S(1)}, u32[]{:S(2)}, u32[]{:S(2)}) collective-permute-start(bf16[4,1,32,2,512]{4,2,3,1,0:T(8,128)(2,1)S(1)} %get-tuple-element.142), channel_id=1, source_target_pairs={{1,0},{2,1},{3,2},{5,4},{6,5},{7,6},{9,8},{10,9},{11,10},{13,12},{... | collective-permute-start | bytes 786440 | tf_op jit(solution)/shard_map/ppermute | solution.py:23
  372.3 8.4 %slice-start = ((s8[9437184]{0:T(1024)(128)(4,1)}), s8[4194304]{0:T(1024)(128)(4,1)S(1)}, s32[]{:S(2)}) async-start(s8[9437184]{0:T(1024)(128)(4,1)} %bitcast.210), calls=%async_computation.2 | async-start | bytes 8388608
  372.3 8.4 %slice-start.1 = ((s8[9437184]{0:T(1024)(128)(4,1)}), s8[4194304]{0:T(1024)(128)(4,1)S(1)}, s32[]{:S(2)}) async-start(s8[9437184]{0:T(1024)(128)(4,1)} %bitcast.210), calls=%async_computation.3 | async-start | bytes 8388608
  374.9 5.8 %slice-start.2 = ((s8[9437184]{0:T(1024)(128)(4,1)}), s8[1048576]{0:T(1024)(128)(4,1)S(1)}, s32[]{:S(2)}) async-start(s8[9437184]{0:T(1024)(128)(4,1)} %bitcast.210), calls=%async_computation.4 | async-start | bytes 2097152
  387.0 2.6 copy-start.2
  387.0 2.6 copy-start.7
Sparse Core Ops, SparseCore 0:
  8.9 165.1 all-gather.2
  175.6 164.9 all-gather.4
where the time goes:
time: 406 us; the launch traced here: 405 us
  waiting for transfers between devices  248 us (61%)
  matrix products  61.8 us (15%)
  starting transfers between devices  41.7 us (10%)
  local copies, waits for them, and re-layouts  21.8 us (5%)
  other arithmetic  17.6 us (4%)
  between operations  13.7 us (3%)
    all_gather x1, waiting for transfers between devices, on_device(): lax.all_gather(weight_in, 'rows', axis=1, tiled=True)  154 us
    ppermute x14, waiting for transfers between devices, passed_along(): lax.ppermute(value, axis, [(source, source + steps) for source in range(f...  89.9 us
    dot_general x9, matrix products, in_term(): lax.dot_general(window, weight_tap, (((3,), (1,)), ((), ())), preferred_e...  37.8 us
    ppermute x14, starting transfers between devices, passed_along(): lax.ppermute(value, axis, [(source, source + steps) for source in range(f...  29.1 us
    dot_general x9, matrix products, out_term(): lax.dot_general(window, piece[tap_index], (((3, 4), (0, 1)), ((), ())), p...  24 us
    dynamic_update_slice x4, other arithmetic, run_states(): lax.scan(advance, (begin_re, begin_im), (driven[..., 0, :], driven[..., 1...  9.82 us
  transfers between devices with their start and end apart: 20, of which 16 were waited for; matrix products, arithmetic and copies ran while one was open for 20% of the time, Pallas kernels for 0%

commit v1 on v0

--- a/solution.py
+++ b/solution.py
@@ -111,7 +111,7 @@
     extended = extended_2(frames_in, (("rows", 1),), 1)
     padded = pad_field(extended, 0)
     driven = in_term(
-        padded, lax.all_gather(weight_in, "rows", axis=1, tiled=True), band_rows, columns
+        padded, jnp.concatenate(lax.all_gather(weight_in, "rows"), axis=1), band_rows, columns
     )
     held = run_states(driven, start_state[:, :, 0, :], start_state[:, :, 1, :], log_decay, rotation)
     held = extended_2(held, (("rows", 1),), 1)

time: 406 us -> 421 us (1.037)
  local copies, waits for them, and re-layouts: 21.8 us -> 29.7 us
  matrix products: 61.8 us -> 68.6 us
    all_gather x0 -> x1, local copies, waits for them, and re-layouts: none -> 7.95 us  [on_device(): lax.all_gather(weight_in, 'rows')]
    dot_general x9, matrix products: 37.8 us -> 44.6 us  [in_term(): lax.dot_general(window, weight_tap, (((3,), (1,)), ((), ())), preferred_e...]
  transfers between devices with their start and end apart: 20 -> 20, of which waited for: 16 -> 16; matrix products, arithmetic and copies ran while one was open for 20% -> 23% of each run, Pallas kernels for 0% -> 0%
where the time goes in v1:
time: 421 us; the launch traced here: 420 us
  waiting for transfers between devices  248 us (59%)
  matrix products  68.6 us (16%)
  starting transfers between devices  41.6 us (10%)
  local copies, waits for them, and re-layouts  29.7 us (7%)
  other arithmetic  17.6 us (4%)
  between operations  13.7 us (3%)
    all_gather x1, waiting for transfers between devices, on_device(): lax.all_gather(weight_in, 'rows')  154 us
    ppermute x14, waiting for transfers between devices, passed_along(): lax.ppermute(value, axis, [(source, source + steps) for source in range(f...  89.9 us
    dot_general x9, matrix products, in_term(): lax.dot_general(window, weight_tap, (((3,), (1,)), ((), ())), preferred_e...  44.6 us
    ppermute x14, starting transfers between devices, passed_along(): lax.ppermute(value, axis, [(source, source + steps) for source in range(f...  29.1 us
    dot_general x9, matrix products, out_term(): lax.dot_general(window, piece[tap_index], (((3, 4), (0, 1)), ((), ())), p...  24 us
    dynamic_update_slice x4, other arithmetic, run_states(): lax.scan(advance, (begin_re, begin_im), (driven[..., 0, :], driven[..., 1...  9.82 us
  transfers between devices with their start and end apart: 20, of which 16 were waited for; matrix products, arithmetic and copies ran while one was open for 23% of the time, Pallas kernels for 0%

profile of v1, /device:TPU:12, one launch (start us, length us, event | category | flops | bytes accessed | tf_op | source)
XLA Modules:
  0.0 419.7 jit_solution(14305211949276130117)
XLA Ops:
  9.0 3.5 collective-permute-start.2
  20.2 153.8 %all-gather.6.cloned.1.call-done = bf16[8,128,4608]{2,1,0:T(8,128)(2,1)} async-done(((bf16[2,128,4608]{2,1,0:T(8,128)(2,1)}), bf16[8,128,4608]{2,1,0:T(8,128)(2,1)}) %all-gather.6.cloned.1.call-update) | async-done | bytes 9437200 | tf_op jit(solution)/shard_map/all_gather | solution.py:114
  174.1 7.9 %copy.16 = bf16[4,2,128,4608]{3,2,0,1:T(8,128)(2,1)} copy(bf16[4,2,128,4608]{3,2,1,0:T(8,128)(2,1)} %bitcast.213) | data formatting | bytes 18874368 | tf_op jit(solution)/shard_map/all_gather | solution.py:114
  182.0 5.4 %fusion.51 = f32[4,8,32,1024]{3,2,1,0:T(8,128)} fusion(bf16[4,8,32,512]{3,2,1,0:T(8,128)(2,1)} %param.11, bf16[4,1,32,512]{3,2,1,0:T(8,128)(2,1)S(1)} %collective-permute-done.2, bf16[1024,4608]{1,0:T(8,128)(2,1)} %bitcast.204), kind=kOutput, calls=%fused_computation.83 | convolution fusion | flops 1076101120 | bytes 6422528 | tf_op jit(solution)/shard_map/dot_general | solution.py:47
  187.4 5.5 %fusion.55 = f32[4,8,32,1024]{3,2,1,0:T(8,128)} fusion(bf16[4,1,32,512]{3,2,1,0:T(8,128)(2,1)S(1)} %collective-permute-done.3, bf16[4,8,32,512]{3,2,1,0:T(8,128)(2,1)} %param.11, bf16[1024,4608]{1,0:T(8,128)(2,1)} %bitcast.205), kind=kOutput, calls=%fused_computation.87 | convolution fusion | flops 1076101120 | bytes 6422528 | tf_op jit(solution)/shard_map/dot_general | solution.py:47
  196.1 3.3 fusion.65
  199.4 3.4 fusion.68
  206.0 3.2 fusion.72
  209.2 3.3 fusion.67
  212.5 14.1 %add_add_fusion.1 = f32[4,8,32,1024]{3,2,1,0:T(8,128)} fusion(f32[4,8,32,1024]{3,2,1,0:T(8,128)} %fusion.55, f32[4,8,32,1024]{3,2,1,0:T(8,128)} %fusion.63, f32[4,8,32,1024]{3,2,1,0:T(8,128)} %fusion.65, f32[4,8,32,1024]{3,2,1,0:T(8,128)} %fusion.67, f32[4,8,32,1024]{3,2,1,0:T(8,128)} %fusion.68, f32[4,8,32,1024]{3,2,1,0:T(8,128)} %fusion.70, ...), kind=kOutput, calls=%fused_computation.11 | convolution fusion | flops 1082130432 | bytes 39845888 | tf_op jit(solution)/shard_map/dot_general | solution.py:47
  226.6 6.6 %reshape.132 = f32[4,8,32,2,512]{4,3,2,1,0:T(2,128)} reshape(f32[4,8,32,1024]{3,2,1,0:T(8,128)} %add_add_fusion.1) | data formatting | bytes 8388608 | tf_op jit(solution)/shard_map/reshape | solution.py:50
  233.2 7.9 %fusion.83 = (f32[4,8,32,1,512]{4,3,2,1,0:T(1,128)S(1)}, f32[4,8,32,1,512]{4,3,2,1,0:T(1,128)S(1)}) fusion(f32[4,8,32,2,512]{4,3,2,1,0:T(2,128)} %reshape.132), kind=kLoop, calls=%fused_computation.146 | loop fusion | bytes 8388608 | tf_op jit(solution)/shard_map/slice | solution.py:85
  246.3 9.8 %while.28 = (s32[]{:T(128)}, f32[8,32,512]{2,1,0:T(8,128)S(1)}, f32[8,32,512]{2,1,0:T(8,128)S(1)}, f32[4,8,32,512]{3,2,1,0:T(8,128)}, f32[4,8,32,512]{3,2,1,0:T(...) while((s32[]{:T(128)}, f32[8,32,512]{2,1,0:T(8,128)S(1)}, ...), condition=%wide.region_1.2_spmd, body=%wide.region_0.1_spmd.sunk | while | flops 1048578 | bytes 4199013 | solution.py:84
  256.2 120.9 %while.29 = (s32[]{:T(128)}, f32[8,32,512]{2,1,0:T(8,128)S(1)}, f32[8,32,512]{2,1,0:T(8,128)S(1)}, f32[512]{0:T(512)S(1)}, f32[512]{0:T(512)S(1)}, /*index=5*/f3...) while((s32[]{:T(128)}, f32[8,32,512]{2,1,0:T(8,128)S(1)}, f32[8,32,512]{2,1,0:T(8,128)S(1)}, ...), condition=%wide.region_3.4_spmd, body=%wide.region_2.3_spmd.sunk | while | flops 1048578 | bytes 7344293 | solution.py:97
  258.4 3.5 collective-permute-start.1
  261.9 6.0 %collective-permute-done = f32[8,32,512]{2,1,0:T(8,128)S(1)} collective-permute-done((f32[8,32,512]{2,1,0:T(8,128)S(1)}, f32[8,32,512]{2,1,0:T(8,128)S(1)}, u32[]{:S(2)}, u32[]{:S(2)}) %collective-permute-start) | collective-permute-done | bytes 524320 | tf_op jit(solution)/shard_map/while/body/eval_jaxpr/ppermute | solution.py:10
  267.9 5.6 %collective-permute-done.1 = f32[8,32,512]{2,1,0:T(8,128)S(1)} collective-permute-done((f32[8,32,512]{2,1,0:T(8,128)S(1)}, f32[8,32,512]{2,1,0:T(8,128)S(1)}, u32[]{:S(2)}, u32[]{:S(2)}) %collective-permute-start.1) | collective-permute-done | bytes 524320 | tf_op jit(solution)/shard_map/while/body/eval_jaxpr/ppermute | solution.py:10
  278.3 6.9 %collective-permute-done = f32[8,32,512]{2,1,0:T(8,128)S(1)} collective-permute-done((f32[8,32,512]{2,1,0:T(8,128)S(1)}, f32[8,32,512]{2,1,0:T(8,128)S(1)}, u32[]{:S(2)}, u32[]{:S(2)}) %collective-permute-start) | collective-permute-done | bytes 524320 | tf_op jit(solution)/shard_map/while/body/eval_jaxpr/ppermute | solution.py:10
  285.2 5.6 %collective-permute-done.1 = f32[8,32,512]{2,1,0:T(8,128)S(1)} collective-permute-done((f32[8,32,512]{2,1,0:T(8,128)S(1)}, f32[8,32,512]{2,1,0:T(8,128)S(1)}, u32[]{:S(2)}, u32[]{:S(2)}) %collective-permute-start.1) | collective-permute-done | bytes 524320 | tf_op jit(solution)/shard_map/while/body/eval_jaxpr/ppermute | solution.py:10
  294.9 7.5 %collective-permute-done = f32[8,32,512]{2,1,0:T(8,128)S(1)} collective-permute-done((f32[8,32,512]{2,1,0:T(8,128)S(1)}, f32[8,32,512]{2,1,0:T(8,128)S(1)}, u32[]{:S(2)}, u32[]{:S(2)}) %collective-permute-start) | collective-permute-done | bytes 524320 | tf_op jit(solution)/shard_map/while/body/eval_jaxpr/ppermute | solution.py:10
  302.4 5.6 %collective-permute-done.1 = f32[8,32,512]{2,1,0:T(8,128)S(1)} collective-permute-done((f32[8,32,512]{2,1,0:T(8,128)S(1)}, f32[8,32,512]{2,1,0:T(8,128)S(1)}, u32[]{:S(2)}, u32[]{:S(2)}) %collective-permute-start.1) | collective-permute-done | bytes 524320 | tf_op jit(solution)/shard_map/while/body/eval_jaxpr/ppermute | solution.py:10
  312.2 7.5 %collective-permute-done = f32[8,32,512]{2,1,0:T(8,128)S(1)} collective-permute-done((f32[8,32,512]{2,1,0:T(8,128)S(1)}, f32[8,32,512]{2,1,0:T(8,128)S(1)}, u32[]{:S(2)}, u32[]{:S(2)}) %collective-permute-start) | collective-permute-done | bytes 524320 | tf_op jit(solution)/shard_map/while/body/eval_jaxpr/ppermute | solution.py:10
  319.7 5.6 %collective-permute-done.1 = f32[8,32,512]{2,1,0:T(8,128)S(1)} collective-permute-done((f32[8,32,512]{2,1,0:T(8,128)S(1)}, f32[8,32,512]{2,1,0:T(8,128)S(1)}, u32[]{:S(2)}, u32[]{:S(2)}) %collective-permute-start.1) | collective-permute-done | bytes 524320 | tf_op jit(solution)/shard_map/while/body/eval_jaxpr/ppermute | solution.py:10
  329.4 7.5 %collective-permute-done = f32[8,32,512]{2,1,0:T(8,128)S(1)} collective-permute-done((f32[8,32,512]{2,1,0:T(8,128)S(1)}, f32[8,32,512]{2,1,0:T(8,128)S(1)}, u32[]{:S(2)}, u32[]{:S(2)}) %collective-permute-start) | collective-permute-done | bytes 524320 | tf_op jit(solution)/shard_map/while/body/eval_jaxpr/ppermute | solution.py:10
  337.0 5.6 %collective-permute-done.1 = f32[8,32,512]{2,1,0:T(8,128)S(1)} collective-permute-done((f32[8,32,512]{2,1,0:T(8,128)S(1)}, f32[8,32,512]{2,1,0:T(8,128)S(1)}, u32[]{:S(2)}, u32[]{:S(2)}) %collective-permute-start.1) | collective-permute-done | bytes 524320 | tf_op jit(solution)/shard_map/while/body/eval_jaxpr/ppermute | solution.py:10
  346.7 7.5 %collective-permute-done = f32[8,32,512]{2,1,0:T(8,128)S(1)} collective-permute-done((f32[8,32,512]{2,1,0:T(8,128)S(1)}, f32[8,32,512]{2,1,0:T(8,128)S(1)}, u32[]{:S(2)}, u32[]{:S(2)}) %collective-permute-start) | collective-permute-done | bytes 524320 | tf_op jit(solution)/shard_map/while/body/eval_jaxpr/ppermute | solution.py:10
  354.3 5.6 %collective-permute-done.1 = f32[8,32,512]{2,1,0:T(8,128)S(1)} collective-permute-done((f32[8,32,512]{2,1,0:T(8,128)S(1)}, f32[8,32,512]{2,1,0:T(8,128)S(1)}, u32[]{:S(2)}, u32[]{:S(2)}) %collective-permute-start.1) | collective-permute-done | bytes 524320 | tf_op jit(solution)/shard_map/while/body/eval_jaxpr/ppermute | solution.py:10
  364.0 7.5 %collective-permute-done = f32[8,32,512]{2,1,0:T(8,128)S(1)} collective-permute-done((f32[8,32,512]{2,1,0:T(8,128)S(1)}, f32[8,32,512]{2,1,0:T(8,128)S(1)}, u32[]{:S(2)}, u32[]{:S(2)}) %collective-permute-start) | collective-permute-done | bytes 524320 | tf_op jit(solution)/shard_map/while/body/eval_jaxpr/ppermute | solution.py:10
  371.5 5.6 %collective-permute-done.1 = f32[8,32,512]{2,1,0:T(8,128)S(1)} collective-permute-done((f32[8,32,512]{2,1,0:T(8,128)S(1)}, f32[8,32,512]{2,1,0:T(8,128)S(1)}, u32[]{:S(2)}, u32[]{:S(2)}) %collective-permute-start.1) | collective-permute-done | bytes 524320 | tf_op jit(solution)/shard_map/while/body/eval_jaxpr/ppermute | solution.py:10
  380.2 4.6 %collective-permute-start.4 = (bf16[4,1,32,2,512]{4,2,3,1,0:T(8,128)(2,1)S(1)}, bf16[4,1,32,2,512]{4,2,3,1,0:T(8,128)(2,1)S(1)}, u32[]{:S(2)}, u32[]{:S(2)}) collective-permute-start(bf16[4,1,32,2,512]{4,2,3,1,0:T(8,128)(2,1)S(1)} %get-tuple-element.141), channel_id=1, source_target_pairs={{0,1},{1,2},{2,3},{4,5},{5,6},{6,7},{8,9},{9,10},{10,11},{12,13},{... | collective-permute-start | bytes 786440 | tf_op jit(solution)/shard_map/ppermute | solution.py:21
  389.6 3.9 fusion.5
  404.3 8.6 %fusion.19 = bf16[4,8,32,512]{3,2,1,0:T(8,128)(2,1)} fusion(bf16[4,8,32,512]{3,2,1,0:T(8,128)(2,1)S(1)} %copy-done.3, f32[4,8,32,512,1]{3,2,4,1,0:T(8,128)} %fusion.11, f32[4,8,32,512,1]{3,2,4,1,0:T(8,128)S(1)} %fusion.22, f32[4,8,32,512,1]{3,2,4,1,0:T(8,128)S(1)} %fusion.24, f32[4,8,32,512,1]{3,2,4,1,0:T(8,128)S(1)} %fusion.32, ...), kind=kOutput, calls=%fused_computation.33 | convolution fusion | flops 1113587712 | bytes 22022144 | tf_op jit(solution)/shard_map/dot_general | solution.py:59
  (82 shorter events, 77.5 us)
Async XLA Ops:
  6.5 8.4 %copy-start.6 = (f32[512]{0:T(512)S(1)}, f32[512]{0:T(512)}, u32[]{:S(2)}) copy-start(f32[512]{0:T(512)} %param.14) | copy-start | bytes 6148
  6.5 8.4 %copy-start.5 = (f32[512]{0:T(512)S(1)}, f32[512]{0:T(512)}, u32[]{:S(2)}) copy-start(f32[512]{0:T(512)} %param.15) | copy-start | bytes 6148
  6.5 8.4 %copy-start.4 = (f32[8,32,2,512]{3,2,1,0:T(2,128)S(1)}, f32[8,32,2,512]{3,2,1,0:T(2,128)}, u32[]{:S(2)}) copy-start(f32[8,32,2,512]{3,2,1,0:T(2,128)} %param.16) | copy-start | bytes 3145732
  6.5 167.5 %all-gather.6.cloned.1.call-start = ((), (), s32[]{:S(2)}) async-start(), calls=%async_computation.1 | async-start | bytes 11796480 | tf_op jit(solution)/shard_map/all_gather | solution.py:114
  7.3 379.7 %all-gather.4.cloned.1.call-start = ((), (), s32[]{:S(2)}) async-start(), calls=%async_computation | async-start | bytes 11796480 | tf_op jit(solution)/shard_map/all_gather | solution.py:120
  9.0 7.3 %collective-permute-start.2 = (bf16[4,1,32,512]{3,2,1,0:T(8,128)(2,1)S(1)}, bf16[4,1,32,512]{3,2,1,0:T(8,128)(2,1)S(1)}, u32[]{:S(2)}, u32[]{:S(2)}) collective-permute-start(bf16[4,1,32,512]{3,2,1,0:T(8,128)(2,1)S(1)} %get-tuple-element.145), channel_id=1, source_target_pairs={{0,1},{1,2},{2,3},{4,5},{5,6},{6,7},{8,9},{9,10},{10,11},{12,13},{... | collective-permute-start | bytes 393224 | tf_op jit(solution)/shard_map/ppermute | solution.py:21
  12.5 6.9 %collective-permute-start.3 = (bf16[4,1,32,512]{3,2,1,0:T(8,128)(2,1)S(1)}, bf16[4,1,32,512]{3,2,1,0:T(8,128)(2,1)S(1)}, u32[]{:S(2)}, u32[]{:S(2)}) collective-permute-start(bf16[4,1,32,512]{3,2,1,0:T(8,128)(2,1)S(1)} %get-tuple-element.146), channel_id=1, source_target_pairs={{1,0},{2,1},{3,2},{5,4},{6,5},{7,6},{9,8},{10,9},{11,10},{13,12},{... | collective-permute-start | bytes 393224 | tf_op jit(solution)/shard_map/ppermute | solution.py:23
  15.0 4.4 %copy-start.1 = (bf16[4,8,32,512]{3,2,1,0:T(8,128)(2,1)S(1)}, bf16[4,8,32,512]{3,2,1,0:T(8,128)(2,1)}, u32[]{:S(2)}) copy-start(bf16[4,8,32,512]{3,2,1,0:T(8,128)(2,1)} %param.11) | copy-start | bytes 3145732
  182.0 10.9 %copy-start = (bf16[4,2,128,4608]{3,2,0,1:T(8,128)(2,1)S(1)}, bf16[4,2,128,4608]{3,2,0,1:T(8,128)(2,1)}, u32[]{:S(2)}) copy-start(bf16[4,2,128,4608]{3,2,0,1:T(8,128)(2,1)} %copy.16) | copy-start | bytes 28311556
  206.0 3.2 copy-start.2
  256.5 11.4 %collective-permute-start = (f32[8,32,512]{2,1,0:T(8,128)S(1)}, f32[8,32,512]{2,1,0:T(8,128)S(1)}, u32[]{:S(2)}, u32[]{:S(2)}) collective-permute-start(f32[8,32,512]{2,1,0:T(8,128)S(1)} %get-tuple-element.268), channel_id=1, source_target_pairs={{0,4},{4,8},{8,12},{12,16},{16,20},{20,24},{24,28},{1,5},{5,9},{9,... | collective-permute-start | bytes 1572872 | tf_op jit(solution)/shard_map/while/body/eval_jaxpr/ppermute | solution.py:10
  258.4 15.1 %collective-permute-start.1 = (f32[8,32,512]{2,1,0:T(8,128)S(1)}, f32[8,32,512]{2,1,0:T(8,128)S(1)}, u32[]{:S(2)}, u32[]{:S(2)}) collective-permute-start(f32[8,32,512]{2,1,0:T(8,128)S(1)} %get-tuple-element.269), channel_id=1, source_target_pairs={{0,4},{4,8},{8,12},{12,16},{16,20},{20,24},{24,28},{1,5},{5,9},{9,... | collective-permute-start | bytes 1572872 | tf_op jit(solution)/shard_map/while/body/eval_jaxpr/ppermute | solution.py:10
  273.8 11.4 %collective-permute-start = (f32[8,32,512]{2,1,0:T(8,128)S(1)}, f32[8,32,512]{2,1,0:T(8,128)S(1)}, u32[]{:S(2)}, u32[]{:S(2)}) collective-permute-start(f32[8,32,512]{2,1,0:T(8,128)S(1)} %get-tuple-element.268), channel_id=1, source_target_pairs={{0,4},{4,8},{8,12},{12,16},{16,20},{20,24},{24,28},{1,5},{5,9},{9,... | collective-permute-start | bytes 1572872 | tf_op jit(solution)/shard_map/while/body/eval_jaxpr/ppermute | solution.py:10
  275.7 15.1 %collective-permute-start.1 = (f32[8,32,512]{2,1,0:T(8,128)S(1)}, f32[8,32,512]{2,1,0:T(8,128)S(1)}, u32[]{:S(2)}, u32[]{:S(2)}) collective-permute-start(f32[8,32,512]{2,1,0:T(8,128)S(1)} %get-tuple-element.269), channel_id=1, source_target_pairs={{0,4},{4,8},{8,12},{12,16},{16,20},{20,24},{24,28},{1,5},{5,9},{9,... | collective-permute-start | bytes 1572872 | tf_op jit(solution)/shard_map/while/body/eval_jaxpr/ppermute | solution.py:10
  291.0 11.4 %collective-permute-start = (f32[8,32,512]{2,1,0:T(8,128)S(1)}, f32[8,32,512]{2,1,0:T(8,128)S(1)}, u32[]{:S(2)}, u32[]{:S(2)}) collective-permute-start(f32[8,32,512]{2,1,0:T(8,128)S(1)} %get-tuple-element.268), channel_id=1, source_target_pairs={{0,4},{4,8},{8,12},{12,16},{16,20},{20,24},{24,28},{1,5},{5,9},{9,... | collective-permute-start | bytes 1572872 | tf_op jit(solution)/shard_map/while/body/eval_jaxpr/ppermute | solution.py:10
  293.0 15.1 %collective-permute-start.1 = (f32[8,32,512]{2,1,0:T(8,128)S(1)}, f32[8,32,512]{2,1,0:T(8,128)S(1)}, u32[]{:S(2)}, u32[]{:S(2)}) collective-permute-start(f32[8,32,512]{2,1,0:T(8,128)S(1)} %get-tuple-element.269), channel_id=1, source_target_pairs={{0,4},{4,8},{8,12},{12,16},{16,20},{20,24},{24,28},{1,5},{5,9},{9,... | collective-permute-start | bytes 1572872 | tf_op jit(solution)/shard_map/while/body/eval_jaxpr/ppermute | solution.py:10
  308.3 11.4 %collective-permute-start = (f32[8,32,512]{2,1,0:T(8,128)S(1)}, f32[8,32,512]{2,1,0:T(8,128)S(1)}, u32[]{:S(2)}, u32[]{:S(2)}) collective-permute-start(f32[8,32,512]{2,1,0:T(8,128)S(1)} %get-tuple-element.268), channel_id=1, source_target_pairs={{0,4},{4,8},{8,12},{12,16},{16,20},{20,24},{24,28},{1,5},{5,9},{9,... | collective-permute-start | bytes 1572872 | tf_op jit(solution)/shard_map/while/body/eval_jaxpr/ppermute | solution.py:10
  310.2 15.1 %collective-permute-start.1 = (f32[8,32,512]{2,1,0:T(8,128)S(1)}, f32[8,32,512]{2,1,0:T(8,128)S(1)}, u32[]{:S(2)}, u32[]{:S(2)}) collective-permute-start(f32[8,32,512]{2,1,0:T(8,128)S(1)} %get-tuple-element.269), channel_id=1, source_target_pairs={{0,4},{4,8},{8,12},{12,16},{16,20},{20,24},{24,28},{1,5},{5,9},{9,... | collective-permute-start | bytes 1572872 | tf_op jit(solution)/shard_map/while/body/eval_jaxpr/ppermute | solution.py:10
  325.6 11.4 %collective-permute-start = (f32[8,32,512]{2,1,0:T(8,128)S(1)}, f32[8,32,512]{2,1,0:T(8,128)S(1)}, u32[]{:S(2)}, u32[]{:S(2)}) collective-permute-start(f32[8,32,512]{2,1,0:T(8,128)S(1)} %get-tuple-element.268), channel_id=1, source_target_pairs={{0,4},{4,8},{8,12},{12,16},{16,20},{20,24},{24,28},{1,5},{5,9},{9,... | collective-permute-start | bytes 1572872 | tf_op jit(solution)/shard_map/while/body/eval_jaxpr/ppermute | solution.py:10
  327.5 15.1 %collective-permute-start.1 = (f32[8,32,512]{2,1,0:T(8,128)S(1)}, f32[8,32,512]{2,1,0:T(8,128)S(1)}, u32[]{:S(2)}, u32[]{:S(2)}) collective-permute-start(f32[8,32,512]{2,1,0:T(8,128)S(1)} %get-tuple-element.269), channel_id=1, source_target_pairs={{0,4},{4,8},{8,12},{12,16},{16,20},{20,24},{24,28},{1,5},{5,9},{9,... | collective-permute-start | bytes 1572872 | tf_op jit(solution)/shard_map/while/body/eval_jaxpr/ppermute | solution.py:10
  342.9 11.4 %collective-permute-start = (f32[8,32,512]{2,1,0:T(8,128)S(1)}, f32[8,32,512]{2,1,0:T(8,128)S(1)}, u32[]{:S(2)}, u32[]{:S(2)}) collective-permute-start(f32[8,32,512]{2,1,0:T(8,128)S(1)} %get-tuple-element.268), channel_id=1, source_target_pairs={{0,4},{4,8},{8,12},{12,16},{16,20},{20,24},{24,28},{1,5},{5,9},{9,... | collective-permute-start | bytes 1572872 | tf_op jit(solution)/shard_map/while/body/eval_jaxpr/ppermute | solution.py:10
  344.8 15.1 %collective-permute-start.1 = (f32[8,32,512]{2,1,0:T(8,128)S(1)}, f32[8,32,512]{2,1,0:T(8,128)S(1)}, u32[]{:S(2)}, u32[]{:S(2)}) collective-permute-start(f32[8,32,512]{2,1,0:T(8,128)S(1)} %get-tuple-element.269), channel_id=1, source_target_pairs={{0,4},{4,8},{8,12},{12,16},{16,20},{20,24},{24,28},{1,5},{5,9},{9,... | collective-permute-start | bytes 1572872 | tf_op jit(solution)/shard_map/while/body/eval_jaxpr/ppermute | solution.py:10
  360.1 11.4 %collective-permute-start = (f32[8,32,512]{2,1,0:T(8,128)S(1)}, f32[8,32,512]{2,1,0:T(8,128)S(1)}, u32[]{:S(2)}, u32[]{:S(2)}) collective-permute-start(f32[8,32,512]{2,1,0:T(8,128)S(1)} %get-tuple-element.268), channel_id=1, source_target_pairs={{0,4},{4,8},{8,12},{12,16},{16,20},{20,24},{24,28},{1,5},{5,9},{9,... | collective-permute-start | bytes 1572872 | tf_op jit(solution)/shard_map/while/body/eval_jaxpr/ppermute | solution.py:10
  362.1 15.1 %collective-permute-start.1 = (f32[8,32,512]{2,1,0:T(8,128)S(1)}, f32[8,32,512]{2,1,0:T(8,128)S(1)}, u32[]{:S(2)}, u32[]{:S(2)}) collective-permute-start(f32[8,32,512]{2,1,0:T(8,128)S(1)} %get-tuple-element.269), channel_id=1, source_target_pairs={{0,4},{4,8},{8,12},{12,16},{16,20},{20,24},{24,28},{1,5},{5,9},{9,... | collective-permute-start | bytes 1572872 | tf_op jit(solution)/shard_map/while/body/eval_jaxpr/ppermute | solution.py:10
  380.2 9.4 %collective-permute-start.4 = (bf16[4,1,32,2,512]{4,2,3,1,0:T(8,128)(2,1)S(1)}, bf16[4,1,32,2,512]{4,2,3,1,0:T(8,128)(2,1)S(1)}, u32[]{:S(2)}, u32[]{:S(2)}) collective-permute-start(bf16[4,1,32,2,512]{4,2,3,1,0:T(8,128)(2,1)S(1)} %get-tuple-element.141), channel_id=1, source_target_pairs={{0,1},{1,2},{2,3},{4,5},{5,6},{6,7},{8,9},{9,10},{10,11},{12,13},{... | collective-permute-start | bytes 786440 | tf_op jit(solution)/shard_map/ppermute | solution.py:21
  384.8 8.7 %collective-permute-start.5 = (bf16[4,1,32,2,512]{4,2,3,1,0:T(8,128)(2,1)S(1)}, bf16[4,1,32,2,512]{4,2,3,1,0:T(8,128)(2,1)S(1)}, u32[]{:S(2)}, u32[]{:S(2)}) collective-permute-start(bf16[4,1,32,2,512]{4,2,3,1,0:T(8,128)(2,1)S(1)} %get-tuple-element.142), channel_id=1, source_target_pairs={{1,0},{2,1},{3,2},{5,4},{6,5},{7,6},{9,8},{10,9},{11,10},{13,12},{... | collective-permute-start | bytes 786440 | tf_op jit(solution)/shard_map/ppermute | solution.py:23
  386.9 8.4 %slice-start = ((s8[9437184]{0:T(1024)(128)(4,1)}), s8[4194304]{0:T(1024)(128)(4,1)S(1)}, s32[]{:S(2)}) async-start(s8[9437184]{0:T(1024)(128)(4,1)} %bitcast.214), calls=%async_computation.2 | async-start | bytes 8388608
  386.9 8.4 %slice-start.1 = ((s8[9437184]{0:T(1024)(128)(4,1)}), s8[4194304]{0:T(1024)(128)(4,1)S(1)}, s32[]{:S(2)}) async-start(s8[9437184]{0:T(1024)(128)(4,1)} %bitcast.214), calls=%async_computation.3 | async-start | bytes 8388608
  389.6 5.8 %slice-start.2 = ((s8[9437184]{0:T(1024)(128)(4,1)}), s8[1048576]{0:T(1024)(128)(4,1)S(1)}, s32[]{:S(2)}) async-start(s8[9437184]{0:T(1024)(128)(4,1)} %bitcast.214), calls=%async_computation.4 | async-start | bytes 2097152
  401.7 2.6 copy-start.3
  401.7 2.6 copy-start.7
Sparse Core Ops, SparseCore 0:
  8.9 165.1 all-gather.5
  175.6 164.9 all-gather.3
